TPU v7x, 32 devices: a whole 2x2x4 slice. The times are simulated.
32 devices in a mesh: dp: 8 (over z, y), tensor: 4 (over x, core).
Axes of the slice: x: 2, y: 2, z: 4, core: 2. Of those that a mesh axis runs over, the one named last changes fastest.
Arguments:
- hidden: bfloat16 [12288, 1536], P('dp'), may hold values from -6 to 6
- segment_ids: int32 [12288], P('dp'), may hold values from -1 to 12287, as said below
- norm_gain: float32 [1536], replicated, may hold values from 0.5 to 1.5
- gate_weight: bfloat16 [1536, 3072], P(None, 'tensor'), may hold values from -0.15625 to 0.15625
- input_weight: bfloat16 [1536, 3072], P(None, 'tensor'), may hold values from -0.15625 to 0.15625
- step_weight: bfloat16 [1536, 48], P(None, 'tensor'), may hold values from -0.15625 to 0.15625
- state_weight: bfloat16 [1536, 256], replicated, may hold values from -0.15625 to 0.15625
- conv_weight: float32 [4, 3072], P(None, 'tensor'), may hold values from -3 to 3
- state_conv_weight: float32 [4, 256], replicated, may hold values from -3 to 3
- conv_bias: float32 [3072], P('tensor'), may hold values from -0.5 to 0.5
- state_conv_bias: float32 [256], replicated, may hold values from -0.5 to 0.5
- step_bias: float32 [48], P('tensor'), may hold values from -6.9 to -2.25
- decay_log: float32 [48], P('tensor'), may hold values from 0 to 2.77
- skip_gain: float32 [48], P('tensor'), may hold values from 0.5 to 1.5
- gate_norm_gain: float32 [3072], P('tensor'), may hold values from 0.5 to 1.5
- out_weight: bfloat16 [3072, 1536], P('tensor'), may hold values from -0.109375 to 0.109375
- cotangent: bfloat16 [12288, 1536], P('dp'), may hold values from -6 to 6
Outputs:
- block_out: bfloat16 [12288, 1536], P('dp')
- grad_hidden: float32 [12288, 1536], P('dp')
- grad_norm_gain: float32 [1536], replicated
- grad_gate_weight: float32 [1536, 3072], P(None, 'tensor')
- grad_input_weight: float32 [1536, 3072], P(None, 'tensor')
- grad_step_weight: float32 [1536, 48], P(None, 'tensor')
- grad_state_weight: float32 [1536, 256], replicated
- grad_conv_weight: float32 [4, 3072], P(None, 'tensor')
- grad_state_conv_weight: float32 [4, 256], replicated
- grad_conv_bias: float32 [3072], P('tensor')
- grad_state_conv_bias: float32 [256], replicated
- grad_step_bias: float32 [48], P('tensor')
- grad_decay_log: float32 [48], P('tensor')
- grad_skip_gain: float32 [48], P('tensor')
- grad_gate_norm_gain: float32 [3072], P('tensor')
- grad_out_weight: float32 [3072, 1536], P('tensor')
Inputs may be any that keep to these rules, and one draw needn't show every extreme that they name: `segment_ids`: each value is -1 for an empty slot or the global index of the first slot of its sequence; a sequence lies within the 1536 slots of one dp index, its slots are consecutive; the empty slots of a dp index come after all its sequences and number a multiple of 256; the last dp index has no empty slot, and the last slot of all starts a sequence of one token.
All inputs are finite; a program needn't handle non-finite values.
Results may differ from a plain program's by a relative error of at most 0.0096.
Values may be sent and summed in bfloat16 or wider, within the bound.
No kernel may reach another device: no remote copies, remote signals or barrier semaphores. Data moves between devices by JAX's collectives and lax.ppermute only.
A program may use at most 256 MiB of HBM per device.

v0:
```python
from functools import partial
import jax
import jax.numpy as jnp
from jax import lax
from jax.sharding import PartitionSpec as P

INNER = 3072
GROUP = 256
EPS = 1e-05
HIGH = lax.Precision.HIGHEST


def conv_silu(inputs, weights, biases, segments):
    summed = biases[None, :] + weights[0][None, :] * inputs
    for offset in range(1, weights.shape[0]):
        shifted = jnp.concatenate(
            [jnp.zeros((offset, inputs.shape[1]), inputs.dtype), inputs[:-offset]], axis=0
        )
        seg_shift = jnp.concatenate([jnp.full((offset,), -2, jnp.int32), segments[:-offset]])
        keeping = (seg_shift == segments).astype(inputs.dtype)
        summed = summed + weights[offset][None, :] * shifted * keeping[:, None]
    return jax.nn.silu(summed)


def ssd_scan(values, states, step_raw, step_bias, decay_log, skip_gain, segments, group):
    length = values.shape[0]
    heads = step_bias.shape[0]
    width = values.shape[1] // heads
    state = states.shape[1] // 2
    blocks = length // group
    step = jax.nn.softplus(step_raw + step_bias[None, :])
    rate = step * (-jnp.exp(decay_log))[None, :]
    x_blk = values.reshape(blocks, group, heads, width)
    b_blk = states[:, :state].reshape(blocks, group, state)
    c_blk = states[:, state:].reshape(blocks, group, state)
    step_h = step.reshape(blocks, group, heads).transpose(0, 2, 1)
    cum_h = jnp.cumsum(rate.reshape(blocks, group, heads), axis=1).transpose(0, 2, 1)
    seg_blk = segments.reshape(blocks, group)
    causal = jnp.tril(jnp.ones((group, group), bool))
    same = ((seg_blk[:, :, None] == seg_blk[:, None, :]) & causal[None])[:, None]
    differ = cum_h[:, :, :, None] - cum_h[:, :, None, :]
    decay = jnp.where(same, jnp.exp(jnp.where(same, differ, 0.0)), 0.0)
    inner_cb = jnp.einsum("cin,cjn->cij", c_blk, b_blk, precision=HIGH)
    mixing = decay * inner_cb[:, None] * step_h[:, :, None, :]
    y_diag = jnp.einsum("chij,cjhp->cihp", mixing, x_blk, precision=HIGH)
    last_seg = seg_blk[:, -1]
    to_end = jnp.exp(cum_h[:, :, -1:] - cum_h) * step_h * (seg_blk == last_seg[:, None])[:, None, :]
    weighted = to_end.transpose(0, 2, 1)[..., None] * x_blk
    local_state = jnp.einsum("cjn,cjhp->chnp", b_blk, weighted, precision=HIGH)
    prev_seg = jnp.concatenate([jnp.full((1,), -3, jnp.int32), last_seg[:-1]])
    carry_keep = (last_seg == prev_seg).astype(values.dtype)[:, None] * jnp.exp(cum_h[:, :, -1])

    def advance(entering, pieces):
        local_part, factor = pieces
        return (local_part + factor[:, None, None] * entering, entering)

    start_state = jnp.zeros((heads, state, width), values.dtype)
    _, entering_all = lax.scan(advance, start_state, (local_state, carry_keep))
    reach = jnp.exp(cum_h).transpose(0, 2, 1) * (seg_blk == prev_seg[:, None])[..., None]
    y_off = jnp.einsum("cin,chnp->cihp", c_blk, entering_all, precision=HIGH) * reach[..., None]
    result = y_diag + y_off + skip_gain[None, None, :, None] * x_blk
    return result.reshape(length, heads * width)


def cross_dot(left, right):
    return lax.dot_general(
        left, right, (((0,), (0,)), ((), ())), preferred_element_type=jnp.float32
    )


def back_dot(left, right):
    return lax.dot_general(
        left, right, (((1,), (1,)), ((), ())), preferred_element_type=jnp.float32
    )


def body(
    hidden,
    segment_ids,
    norm_gain,
    gate_weight,
    input_weight,
    step_weight,
    state_weight,
    conv_weight,
    state_conv_weight,
    conv_bias,
    state_conv_bias,
    step_bias,
    decay_log,
    skip_gain,
    gate_norm_gain,
    out_weight,
    cotangent,
):
    valid = (segment_ids >= 0).astype(jnp.float32)[:, None]
    hidden_f = hidden.astype(jnp.float32)
    inverse = lax.rsqrt(jnp.mean(hidden_f * hidden_f, axis=1, keepdims=True) + EPS)
    normed = (hidden_f * inverse * norm_gain[None, :]).astype(jnp.bfloat16)
    gate_pre = jnp.dot(normed, gate_weight, preferred_element_type=jnp.float32)
    input_pre = jnp.dot(normed, input_weight, preferred_element_type=jnp.float32)
    step_pre = jnp.dot(normed, step_weight, preferred_element_type=jnp.float32)
    state_pre = jnp.dot(normed, state_weight, preferred_element_type=jnp.float32)
    conv_out, conv_back = jax.vjp(
        partial(conv_silu, segments=segment_ids), input_pre, conv_weight, conv_bias
    )
    state_out, state_back = jax.vjp(
        partial(conv_silu, segments=segment_ids), state_pre, state_conv_weight, state_conv_bias
    )
    values_f = lax.optimization_barrier(conv_out.astype(jnp.bfloat16)).astype(jnp.float32)
    states_f = lax.optimization_barrier(state_out.astype(jnp.bfloat16)).astype(jnp.float32)
    mixed_y, ssd_back = jax.vjp(
        partial(ssd_scan, segments=segment_ids, group=GROUP),
        values_f,
        states_f,
        step_pre,
        step_bias,
        decay_log,
        skip_gain,
    )
    gate_act = jax.nn.silu(gate_pre)
    gated = mixed_y * gate_act
    square_sum = lax.psum(jnp.sum(gated * gated, axis=1), "tensor")
    gate_inverse = lax.rsqrt(square_sum / INNER + EPS)[:, None]
    gnormed = (gated * gate_inverse * gate_norm_gain[None, :]).astype(jnp.bfloat16)
    partial_mix = jnp.dot(gnormed, out_weight, preferred_element_type=jnp.float32)
    mix = lax.psum(partial_mix, "tensor")
    block_out = (hidden_f + valid * mix).astype(jnp.bfloat16)
    dmix = (cotangent.astype(jnp.float32) * valid).astype(jnp.bfloat16)
    grad_out = cross_dot(gnormed, dmix)
    d_gn = back_dot(dmix, out_weight)
    grad_gnorm = jnp.sum(d_gn * gated * gate_inverse, axis=0)
    scaled = d_gn * gate_norm_gain[None, :]
    dot_sum = lax.psum(jnp.sum(gated * scaled, axis=1), "tensor")
    d_gated = gate_inverse * scaled - gated * gate_inverse**3 * (dot_sum / INNER)[:, None]
    d_y = d_gated * gate_act
    sigma = jax.nn.sigmoid(gate_pre)
    d_gate = d_gated * mixed_y * sigma * (1.0 + gate_pre * (1.0 - sigma))
    d_values, d_states, d_step, grad_sbias, grad_decay, grad_skip = ssd_back(d_y)
    d_input, grad_conv, grad_cbias = conv_back(d_values)
    gate_b = d_gate.astype(jnp.bfloat16)
    input_b = d_input.astype(jnp.bfloat16)
    step_b = d_step.astype(jnp.bfloat16)
    local_back = (
        back_dot(gate_b, gate_weight)
        + back_dot(input_b, input_weight)
        + back_dot(step_b, step_weight)
    )
    summed_back, states_full = lax.psum((local_back, d_states), "tensor")
    d_state_pre, grad_sconv, grad_scbias = state_back(states_full)
    state_b = d_state_pre.astype(jnp.bfloat16)
    d_normed = summed_back + back_dot(state_b, state_weight)
    grad_norm = jnp.sum(d_normed * hidden_f * inverse, axis=0)
    scaled_in = d_normed * norm_gain[None, :]
    grad_hidden = (
        cotangent.astype(jnp.float32)
        + inverse * scaled_in
        - hidden_f * inverse**3 * jnp.mean(hidden_f * scaled_in, axis=1, keepdims=True)
    )
    grad_gate = cross_dot(normed, gate_b)
    grad_input = cross_dot(normed, input_b)
    grad_step = cross_dot(normed, step_b)
    grad_state = cross_dot(normed, state_b)
    summed = lax.psum(
        (
            grad_norm,
            grad_gate,
            grad_input,
            grad_step,
            grad_state,
            grad_conv,
            grad_sconv,
            grad_cbias,
            grad_scbias,
            grad_sbias,
            grad_decay,
            grad_skip,
            grad_gnorm,
            grad_out,
        ),
        "dp",
    )
    (
        grad_norm,
        grad_gate,
        grad_input,
        grad_step,
        grad_state,
        grad_conv,
        grad_sconv,
        grad_cbias,
        grad_scbias,
        grad_sbias,
        grad_decay,
        grad_skip,
        grad_gnorm,
        grad_out,
    ) = summed
    return (
        block_out,
        grad_hidden,
        grad_norm,
        grad_gate,
        grad_input,
        grad_step,
        grad_state,
        grad_conv,
        grad_sconv,
        grad_cbias,
        grad_scbias,
        grad_sbias,
        grad_decay,
        grad_skip,
        grad_gnorm,
        grad_out,
    )


def solution(mesh):
    return jax.shard_map(
        body,
        mesh=mesh,
        in_specs=(
            P("dp", None),
            P("dp"),
            P(),
            P(None, "tensor"),
            P(None, "tensor"),
            P(None, "tensor"),
            P(),
            P(None, "tensor"),
            P(),
            P("tensor"),
            P(),
            P("tensor"),
            P("tensor"),
            P("tensor"),
            P("tensor"),
            P("tensor", None),
            P("dp", None),
        ),
        out_specs=(
            P("dp", None),
            P("dp", None),
            P(),
            P(None, "tensor"),
            P(None, "tensor"),
            P(None, "tensor"),
            P(),
            P(None, "tensor"),
            P(),
            P("tensor"),
            P(),
            P("tensor"),
            P("tensor"),
            P("tensor"),
            P("tensor"),
            P("tensor", None),
        ),
        check_vma=False,
    )
```

profile of v0, /device:TPU:0, one launch (start us, length us, event | category | flops | bytes accessed | tf_op | source)
XLA Modules:
  0.0 1345.6 jit_solution(4326663023551138808)
XLA Ops:
  14.4 4.0 fusion.117
  19.1 6.8 multiply_convert_fusion.2
  25.9 8.5 reshape.327
  34.3 8.2 reshape.326
  43.2 4.3 compare_select_fusion.2
  51.8 9.9 copy.178
  61.7 3.8 fusion.118
  71.5 3.8 fusion.67
  78.2 42.7 %while.34 = (s32[]{:T(128)}, f32[12,128,64]{2,1,0:T(8,128)}, f32[6,12,128,64]{3,2,1,0:T(8,128)}, f32[6,12,1,1]{1,3,2,0:T(1,128)}, f32[6,12,128,64]{2,3,1,0:T(8,128)}, /*index=5*/f32[6,12]{1,0:T(8,128)}, s32[]{:T(128)}, s32[]{:T(128)}) while((s32[]{:T(128)}, f32[12,128,64]{2,1,0:T(8,128)}, f32[6,12,128,64]{3,2,1,0:T(8,128)}, ...), condition=%wide.region_4.5_spmd.clone, body=%wide.region_3.4_spmd.clone.sunk | while | flops 393219 | bytes 4327672 | solution.py:58
  120.9 5.4 copy.180
  126.3 5.9 fusion.120
  133.8 7.4 copy.176
  142.3 18.5 %fusion.40 = f32[6,256,12,64]{1,3,2,0:T(8,128)} fusion(f32[6,256,12,64]{1,3,2,0:T(8,128)} %copy.178, f32[6,256,12,64]{1,3,2,0:T(8,128)} %bitcast.225, f32[12]{0:T(128)S(1)} %copy-done.91, f32[6,256,12]{1,2,0:T(8,128)S(1)} %copy-done.30, bf16[6,256,12,64]{1,3,2,0:T(8,128)(2,1)} %copy.176, f32[6,12,256]{2,1,0:T(8,128)S(1)} %bitcast.258, ...), kind=kOutput, calls=%fused_computation.68 | convolution fusion | flops 3652190208 | bytes 18702384 | tf_op jit(solution)/shard_map/jvp(chij,cjhp->cihp)/dot_general | solution.py:45
  160.7 10.7 copy.219
  171.5 9.9 reshape.328
  181.4 10.2 multiply_reduce_fusion.11
  191.7 8.5 psum.133
  200.2 11.6 multiply_reduce_fusion.2
  211.8 6.0 psum.135
  217.9 12.3 multiply_reduce_fusion.3
  230.1 6.1 copy.185
  236.2 6.9 reshape.302
  243.1 19.8 %fusion.77 = f32[6,256,128]{2,1,0:T(8,128)} fusion(f32[6,12,128,64]{3,2,1,0:T(8,128)} %get-tuple-element.547, f32[6,256,12]{1,2,0:T(8,128)S(1)} %copy-done.30, f32[6,256,12,64]{1,0,3,2:T(8,128)} %reshape.302), kind=kOutput, calls=%fused_computation.129 | convolution fusion | flops 1813118976 | bytes 7938048 | tf_op jit(solution)/shard_map/transpose(jvp(cin,chnp->cihp))/dot_general | solution.py:60
  262.9 5.1 multiply_reduce_fusion.8
  268.0 4.9 fusion.70
  276.3 45.5 %while.35 = (s32[]{:T(128)}, f32[12,128,64]{2,1,0:T(8,128)}, f32[6,12,128,64]{3,2,1,0:T(8,128)}, f32[6,12]{1,0:T(8,128)}, f32[6,12,128,64]{2,3,1,0:T(8,128)}, /*...) while((s32[]{:T(128)}, f32[12,128,64]{2,1,0:T(8,128)}, ...), condition=%wide.region_12.13_spmd.clone, body=%wide.region_10.12_spmd.clone.sunk | while | flops 589816 | bytes 4719024 | solution.py:58
  321.8 18.7 %fusion.80 = f32[6,256,128]{2,1,0:T(8,128)S(1)} fusion(f32[6,12,128,64]{3,2,1,0:T(8,128)} %get-tuple-element.193, f32[6,256,12,64]{1,3,2,0:T(8,128)} %copy.178, f32[6,256,12]{1,2,0:T(8,128)} %copy-done.28), kind=kOutput, calls=%fused_computation.130 | convolution fusion | flops 1813118976 | bytes 7938048 | tf_op jit(solution)/shard_map/transpose(jvp(cjn,cjhp->chnp))/dot_general | solution.py:49
  340.6 8.7 multiply_reduce_fusion.9
  349.4 6.8 fusion.106
  356.2 23.7 %fusion.11 = (f32[6,12,256]{2,1,0:T(8,128)}, f32[6,12,256]{2,1,0:T(8,128)}, f32[6,12,256]{2,1,0:T(8,128)}, f32[6,256,256]{2,1,0:T(8,128)S(1)}) fusion(f32[6,12,256]{2,1,0:T(8,128)S(1)} %bitcast.259, f32[6,256,256]{2,1,0:T(8,128)S(1)} %copy-done.26, f32[6,12,256]{2,1,0:T(8,128)S(1)} %copy-done.25, pred[6,256,256]{2,1,0:T(8,128)(4,1)S(1)} %copy-done.35, ...), kind=kOutput, calls=%fused_computation.31 | convolution fusion | flops 3694209024 | bytes 10985472 | tf_op jit(solution)/shard_map/transpose(jvp(chij,cjhp->cihp))/dot_general | solution.py:45
  386.4 14.9 %reduce-window.16 = f32[6,12,2,128]{3,1,2,0:T(8,128)S(1)} reduce-window(f32[6,12,2,128]{3,1,2,0:T(8,128)S(1)} %copy.201, f32[]{:T(128)} %constant.111.clone.1), window={size=1x1x1x128 pad=0_0x0_0x0_0x0_127}, to_apply=%region_19.20 | reduce-window | flops 2340864 | bytes 147460 | tf_op jit(solution)/shard_map/reduce-window.2
  401.9 24.5 %bitcast_add_fusion.2 = f32[6,256,12,64]{1,3,2,0:T(8,128)} fusion(f32[6,256,12,64]{1,3,2,0:T(8,128)} %get-tuple-element.428, f32[12]{0:T(128)} %param.34, f32[6,256,12]{1,2,0:T(8,128)S(1)} %copy-done.29, f32[6,12,256]{2,1,0:T(8,128)} %bitcast.257, f32[6,256,256]{2,1,0:T(8,128)} %fusion.119, f32[6,12,256]{2,1,0:T(8,128)S(1)} %copy-done.25, ...), kind=kOutput, calls=%fused_computation.62 | convolution fusion | flops 3652190208 | bytes 21061680 | tf_op jit(solution)/shard_map/transpose(jvp(chij,cjhp->cihp))/dot_general | solution.py:45
  426.4 10.7 copy.221
  437.2 10.0 reshape.329
  447.2 9.5 multiply_reduce_fusion.7
  465.4 6.5 fusion.122
  472.0 4.0 fusion.121
  477.5 5.1 convolution_add_fusion.1
  482.9 3.9 fusion.97
  486.8 9.4 fusion.124
  496.2 8.7 fusion.123
  504.9 6.7 fusion.63
  511.6 318.8 %all-reduce.34.cloned.1.call-done = (f32[1536,1536]{1,0:T(8,128)}, f32[1536,1536]{1,0:T(8,128)}, f32[1536,256]{1,0:T(8,128)}) async-done(((f32[1536,1536]{1,0:T(8,128)}, f32[1536,1536]{1,0:T(8,128)}, f32[1536,256]{1,0:T(8,128)}), (f32[1536,1536]{1,0:T(8,128)}, f32[1536,1536]{1,0:T(8,128)}, f32[1536,256]{1,0:T(8,128)})) %all-reduce.34.cloned.1.call-update) | async-done | bytes 20447248 | tf_op jit(solution)/shard_map/psum | solution.py:127
  841.0 9.4 fusion.21
  850.4 40.7 %all-reduce.26 = (f32[1536]{0:T(1024)}, f32[4,768]{1,0:T(4,128)}, f32[4,256]{1,0:T(4,128)}, f32[768]{0:T(1024)}, f32[256]{0:T(256)}, /*index=5*/f32[12]{0:T(128)}, f32[12]{0:T(128)}, f32[12]{0:T(128)}, f32[768]{0:T(1024)}) all-reduce(f32[1536]{0:T(1024)S(1)} %get-tuple-element.309, ...), channel_id=1, replica_groups=mesh['dp'=8,'tensor'=4] {'dp'}, use_global_device_ids=true, to_apply=%region_26.27 | all-reduce | flops 7460 | bytes 59680 | tf_op jit(solution)/shard_map/psum | solution.py:164
  891.1 17.0 %fusion.13 = (f32[1536,1536]{1,0:T(8,128)}, bf16[1536,1536]{1,0:T(8,128)(2,1)}) fusion(bf16[1536,1536]{1,0:T(8,128)(2,1)} %param.37, bf16[1536,1536]{1,0:T(8,128)(2,1)} %param.21, f32[1536,1536]{1,0:T(8,128)} %get-tuple-element.429, f32[1536]{0:T(1024)S(1)} %broadcast_multiply_fusion.8, f32[1536]{0:T(1024)S(1)} %copy-done.68, f32[1536]{0:T(1024)S(1)} %copy-done.55, ...), kind=kLoop, calls=%fused_computation.35 | loop fusion | flops 25952256 | bytes 42498048 | tf_op jit(solution)/shard_map/sub | solution.py:156
  908.1 418.2 %all-reduce.32.cloned.1.call-done = (f32[1536,768]{1,0:T(8,128)}, f32[1536,768]{1,0:T(8,128)}, f32[1536,12]{0,1:T(8,128)}, f32[1536,256]{1,0:T(8,128)}, f32[768,1536]{1,0:T(8,128)}) async-done(((f32[1536,768]{1,0:T(8,128)}, f32[1536,768]{1,0:T(8,128)}, f32[1536,12]{0,1:T(8,128)}, f32[1536,256]{1,0:T(8,128)}, f32[768,1536]{1,0:T(8,128)}), (f32[1536,768]{1,0:T(8,128)}, f32[1536,768]{1,0:T(8,128)}, ...) | async-done | bytes 15802384 | tf_op jit(solution)/shard_map/psum | solution.py:164
  1326.3 5.2 copy.308
  (400 shorter events, 150.2 us)
Async XLA Ops:
  7.2 174.3 %copy-start = (bf16[1536,768]{1,0:T(8,128)(2,1)S(1)}, bf16[1536,768]{1,0:T(8,128)(2,1)}, u32[]{:S(2)}) copy-start(bf16[1536,768]{1,0:T(8,128)(2,1)} %param.24) | copy-start | bytes 7077892
  7.2 823.2 %all-reduce.34.cloned.1.call-start = ((), (), s32[]{:S(2)}) async-start(), calls=%async_computation.1 | async-start | bytes 40894464 | tf_op jit(solution)/shard_map/psum | solution.py:127
  18.4 7.5 copy-start.1
  19.1 46.5 %copy-start.37 = (f32[1536]{0:T(1024)}, f32[1536]{0:T(1024)S(1)}, u32[]{:S(2)}) copy-start(f32[1536]{0:T(1024)S(1)} %get-tuple-element.415) | copy-start | bytes 18436
  19.1 46.5 %copy-start.39 = (f32[1536]{0:T(1024)}, f32[1536]{0:T(1024)S(1)}, u32[]{:S(2)}) copy-start(f32[1536]{0:T(1024)S(1)} %get-tuple-element.413) | copy-start | bytes 18436
  19.1 46.5 %copy-start.41 = (f32[1536]{0:T(1024)}, f32[1536]{0:T(1024)S(1)}, u32[]{:S(2)}) copy-start(f32[1536]{0:T(1024)S(1)} %get-tuple-element.414) | copy-start | bytes 18436
  34.3 8.8 copy-start.92
  34.3 8.8 copy-start.45
  34.3 8.9 copy-start.87
  51.6 19.3 %copy-start.23 = (f32[6,12,256]{2,1,0:T(8,128)}, f32[6,12,256]{2,1,0:T(8,128)S(1)}, u32[]{:S(2)}) copy-start(f32[6,12,256]{2,1,0:T(8,128)S(1)} %reduce_window_sum.39) | copy-start | bytes 221188
  51.8 19.1 %copy-start.17 = (f32[6,256,12]{1,0,2:T(8,128)}, f32[6,256,12]{1,0,2:T(8,128)S(1)}, u32[]{:S(2)}) copy-start(f32[6,256,12]{1,0,2:T(8,128)S(1)} %reshape.299) | copy-start | bytes 221188
  51.8 9.9 copy-start.31
  69.1 9.0 copy-start.10
  70.0 8.1 copy-start.49
  70.0 8.1 copy-start.58
  70.2 8.0 copy-start.80
  133.7 7.4 copy-start.36
  133.7 8.5 copy-start.24
  133.7 8.5 copy-start.30
  133.7 8.5 copy-start.51
  133.8 8.5 copy-start.91
  181.4 18.8 %copy-start.44 = (f32[768]{0:T(1024)S(1)}, f32[768]{0:T(1024)}, u32[]{:S(2)}) copy-start(f32[768]{0:T(1024)} %param.35) | copy-start | bytes 9220
  181.4 18.8 %copy-start.56 = (f32[1536]{0:T(1024)S(1)}, f32[1536]{0:T(1024)}, u32[]{:S(2)}) copy-start(f32[1536]{0:T(1024)} %get-tuple-element.412) | copy-start | bytes 18436
  243.1 19.8 %copy-start.4 = (f32[6,256,12,64]{1,0,3,2:T(8,128)S(1)}, f32[6,256,12,64]{1,0,3,2:T(8,128)}, u32[]{:S(2)}) copy-start(f32[6,256,12,64]{1,0,3,2:T(8,128)} %reshape.302) | copy-start | bytes 14155780
  321.8 18.7 %copy-start.7 = (f32[6,12,128,64]{3,2,1,0:T(8,128)S(1)}, f32[6,12,128,64]{3,2,1,0:T(8,128)}, u32[]{:S(2)}) copy-start(f32[6,12,128,64]{3,2,1,0:T(8,128)} %get-tuple-element.193) | copy-start | bytes 7077892
  321.8 18.7 %copy-start.12 = (bf16[1536,128]{1,0:T(8,128)(2,1)S(1)}, bf16[1536,128]{1,0:T(8,128)(2,1)}, u32[]{:S(2)}) copy-start(bf16[1536,128]{1,0:T(8,128)(2,1)} %copy-done.10) | copy-start | bytes 1179652
  321.8 27.5 %slice-start.12 = ((s8[4718592]{0:T(1024)(128)(4,1)}), s8[4194304]{0:T(1024)(128)(4,1)S(1)}, s32[]{:S(2)}) async-start(s8[4718592]{0:T(1024)(128)(4,1)} %bitcast.229), calls=%async_computation.14 | async-start | bytes 8388608
  340.5 8.8 slice-start.13
  340.5 8.8 copy-start.89
  340.6 15.6 %slice-start.2 = ((s8[6291456]{0:T(1024)(128)(4,1)}), s8[4194304]{0:T(1024)(128)(4,1)S(1)}, s32[]{:S(2)}) async-start(s8[6291456]{0:T(1024)(128)(4,1)} %bitcast.216), calls=%async_computation.4 | async-start | bytes 8388608
  356.2 23.7 %copy-start.14 = (f32[6,256,128]{2,1,0:T(8,128)S(1)}, f32[6,256,128]{2,1,0:T(8,128)}, u32[]{:S(2)}) copy-start(f32[6,256,128]{2,1,0:T(8,128)} %fusion.77) | copy-start | bytes 2359300
  356.2 25.5 %copy-start.9 = (bf16[1536,128]{1,0:T(8,128)(2,1)S(1)}, bf16[1536,128]{1,0:T(8,128)(2,1)}, u32[]{:S(2)}) copy-start(bf16[1536,128]{1,0:T(8,128)(2,1)} %get-tuple-element.400) | copy-start | bytes 1179652
  380.0 22.0 %copy-start.29 = (f32[6,256,12]{1,2,0:T(8,128)S(1)}, f32[6,256,12]{1,2,0:T(8,128)}, u32[]{:S(2)}) copy-start(f32[6,256,12]{1,2,0:T(8,128)} %copy-done.28) | copy-start | bytes 221188
  437.2 10.0 copy-start.38
  437.2 19.6 %slice-start = ((s8[4718592]{0:T(1024)(128)(4,1)}), s8[524288]{0:T(1024)(128)(4,1)S(1)}, s32[]{:S(2)}) async-start(s8[4718592]{0:T(1024)(128)(4,1)} %bitcast.205), calls=%async_computation.2 | async-start | bytes 1048576
  447.2 9.6 slice-start.1
  447.2 9.6 copy-start.40
  447.2 9.6 copy-start.42
  482.6 843.6 %all-reduce.32.cloned.1.call-start = ((), (), s32[]{:S(2)}) async-start(), calls=%async_computation | async-start | bytes 31653888 | tf_op jit(solution)/shard_map/psum | solution.py:164
  486.8 9.4 copy-start.21
  486.8 18.1 %slice-start.8 = ((s8[4718592]{0:T(1024)(128)(4,1)}), s8[4194304]{0:T(1024)(128)(4,1)S(1)}, s32[]{:S(2)}) async-start(s8[4718592]{0:T(1024)(128)(4,1)} %bitcast.223), calls=%async_computation.10 | async-start | bytes 8388608
  486.8 18.1 %slice-start.14 = ((s8[4718592]{0:T(1024)(128)(4,1)}), s8[4194304]{0:T(1024)(128)(4,1)S(1)}, s32[]{:S(2)}) async-start(s8[4718592]{0:T(1024)(128)(4,1)} %bitcast.231), calls=%async_computation.16 | async-start | bytes 8388608
  496.2 8.7 slice-start.9
  496.2 8.7 slice-start.15
  496.2 8.7 copy-start.57
  841.0 9.4 copy-start.85
  841.0 50.1 %copy-start.68 = (f32[1536]{0:T(1024)S(1)}, f32[1536]{0:T(1024)}, u32[]{:S(2)}) copy-start(f32[1536]{0:T(1024)} %get-tuple-element.408) | copy-start | bytes 18436
  1326.3 10.0 slice-start.16
  (66 other events, 261.8 us)
Sparse Core Ops, SparseCore 0:
  482.8 347.5 all-reduce.33
  840.2 486.0 all-reduce.31
where the time goes:
time: 1350 us
  waiting for transfers between devices  737 us (55%)
  matrix products  231 us (17%)
  local copies, waits for them, and re-layouts  161 us (12%)
  other arithmetic  145 us (11%)
  blocking collectives  55.2 us (4%)
  between operations  15.8 us (1%)
    psum x1, waiting for transfers between devices, body(): lax.psum((grad_norm, grad_gate, grad_input, grad_step, grad_state, grad_c...  418 us
    psum x1, waiting for transfers between devices, body(): mix = lax.psum(partial_mix, 'tensor')  319 us
    dot_general x3, matrix products, ssd_scan(): y_diag = jnp.einsum('chij,cjhp->cihp', mixing, x_blk, precision=HIGH)  66.6 us
    reshape x6, local copies, waits for them, and re-layouts, ssd_scan(): x_blk = values.reshape(blocks, group, heads, width)  54.7 us
    psum x1, blocking collectives, body(): lax.psum((grad_norm, grad_gate, grad_input, grad_step, grad_state, grad_c...  40.7 us
    dot_general x5, matrix products, back_dot(): lax.dot_general(left, right, (((1,), (1,)), ((), ())), preferred_element_...  36.6 us
    dot_general x3, matrix products, ssd_scan(): local_state = jnp.einsum('cjn,cjhp->chnp', b_blk, weighted, precision=HIGH)  31.2 us
    dot_general x5, matrix products, cross_dot(): lax.dot_general(left, right, (((0,), (0,)), ((), ())), preferred_element_...  31.2 us
  transfers between devices with their start and end apart: 2, of which 2 were waited for; matrix products, arithmetic and copies ran while one was open for 4% of the time, Pallas kernels for 0%

commit v1 on v0

--- a/solution.py
+++ b/solution.py
@@ -124,7 +124,7 @@
     gate_inverse = lax.rsqrt(square_sum / INNER + EPS)[:, None]
     gnormed = (gated * gate_inverse * gate_norm_gain[None, :]).astype(jnp.bfloat16)
     partial_mix = jnp.dot(gnormed, out_weight, preferred_element_type=jnp.float32)
-    mix = lax.psum(partial_mix, "tensor")
+    mix = jnp.sum(lax.all_gather(partial_mix, "tensor"), axis=0)
     block_out = (hidden_f + valid * mix).astype(jnp.bfloat16)
     dmix = (cotangent.astype(jnp.float32) * valid).astype(jnp.bfloat16)
     grad_out = cross_dot(gnormed, dmix)

time: 1350 us -> 1420 us (1.052)
  waiting for transfers between devices: 737 us -> 780 us
  other arithmetic: 145 us -> 164 us
    all_gather x0 -> x1, waiting for transfers between devices: none -> 164 us  [body(): mix = jnp.sum(lax.all_gather(partial_mix, 'tensor'), axis=0)]
    psum x1, waiting for transfers between devices: 319 us -> 160 us  [body(): summed_back, states_full = lax.psum((local_back, d_states), 'tensor')]
    psum x1, waiting for transfers between devices: 418 us -> 455 us  [body(): lax.psum((grad_norm, grad_gate, grad_input, grad_step, grad_state, grad_c...]
    reduce_sum x0 -> x1, other arithmetic: none -> 19.6 us  [body(): mix = jnp.sum(lax.all_gather(partial_mix, 'tensor'), axis=0)]
  transfers between devices with their start and end apart: 2 -> 3, of which waited for: 2 -> 3; matrix products, arithmetic and copies ran while one was open for 4% -> 7% of each run, Pallas kernels for 0% -> 0%
where the time goes in v1:
time: 1420 us; the launch traced here: 1410 us
  waiting for transfers between devices  780 us (55%)
  matrix products  236 us (17%)
  other arithmetic  164 us (12%)
  local copies, waits for them, and re-layouts  161 us (11%)
  blocking collectives  53.4 us (4%)
  between operations  15.6 us (1%)
    psum x1, waiting for transfers between devices, body(): lax.psum((grad_norm, grad_gate, grad_input, grad_step, grad_state, grad_c...  455 us
    all_gather x1, waiting for transfers between devices, body(): mix = jnp.sum(lax.all_gather(partial_mix, 'tensor'), axis=0)  164 us
    psum x1, waiting for transfers between devices, body(): summed_back, states_full = lax.psum((local_back, d_states), 'tensor')  160 us
    dot_general x3, matrix products, ssd_scan(): y_diag = jnp.einsum('chij,cjhp->cihp', mixing, x_blk, precision=HIGH)  66.8 us
    reshape x6, local copies, waits for them, and re-layouts, ssd_scan(): x_blk = values.reshape(blocks, group, heads, width)  54.6 us
    dot_general x5, matrix products, back_dot(): lax.dot_general(left, right, (((1,), (1,)), ((), ())), preferred_element_...  42.5 us
    psum x1, blocking collectives, body(): lax.psum((grad_norm, grad_gate, grad_input, grad_step, grad_state, grad_c...  38.7 us
    dot_general x3, matrix products, ssd_scan(): local_state = jnp.einsum('cjn,cjhp->chnp', b_blk, weighted, precision=HIGH)  31.2 us
  transfers between devices with their start and end apart: 3, of which 3 were waited for; matrix products, arithmetic and copies ran while one was open for 7% of the time, Pallas kernels for 0%

profile of v1, /device:TPU:0, one launch (start us, length us, event | category | flops | bytes accessed | tf_op | source)
XLA Modules:
  0.0 1410.6 jit_solution(17556672709392373257)
XLA Ops:
  14.4 4.0 fusion.117
  19.1 6.4 multiply_convert_fusion.2
  25.5 8.5 reshape.328
  34.0 8.2 reshape.327
  42.9 4.3 compare_select_fusion.2
  51.4 9.9 copy.178
  77.8 42.6 %while.34 = (s32[]{:T(128)}, f32[12,128,64]{2,1,0:T(8,128)}, f32[6,12,128,64]{3,2,1,0:T(8,128)}, f32[6,12,1,1]{1,3,2,0:T(1,128)}, f32[6,12,128,64]{2,3,1,0:T(8,128)}, /*index=5*/f32[6,12]{1,0:T(8,128)}, s32[]{:T(128)}, s32[]{:T(128)}) while((s32[]{:T(128)}, f32[12,128,64]{2,1,0:T(8,128)}, f32[6,12,128,64]{3,2,1,0:T(8,128)}, ...), condition=%wide.region_4.5_spmd.clone, body=%wide.region_3.4_spmd.clone.sunk | while | flops 393219 | bytes 4327672 | solution.py:58
  120.4 5.4 copy.180
  125.9 5.9 fusion.120
  133.3 7.4 copy.176
  141.8 18.5 %fusion.40 = f32[6,256,12,64]{1,3,2,0:T(8,128)} fusion(f32[6,256,12,64]{1,3,2,0:T(8,128)} %copy.178, f32[6,256,12,64]{1,3,2,0:T(8,128)} %bitcast.229, f32[12]{0:T(128)S(1)} %copy-done.90, f32[6,256,12]{1,2,0:T(8,128)S(1)} %copy-done.30, bf16[6,256,12,64]{1,3,2,0:T(8,128)(2,1)} %copy.176, f32[6,12,256]{2,1,0:T(8,128)S(1)} %bitcast.260, ...), kind=kOutput, calls=%fused_computation.68 | convolution fusion | flops 3652190208 | bytes 18702384 | tf_op jit(solution)/shard_map/jvp(chij,cjhp->cihp)/dot_general | solution.py:45
  160.3 10.7 copy.219
  171.0 9.9 reshape.329
  181.0 10.3 multiply_reduce_fusion.11
  191.2 8.5 psum.126
  199.8 11.6 multiply_reduce_fusion.2
  211.3 6.2 psum.127
  217.6 12.3 multiply_reduce_fusion.3
  229.9 6.1 copy.185
  235.9 6.9 reshape.302
  242.8 19.6 %fusion.77 = f32[6,256,128]{2,1,0:T(8,128)} fusion(f32[6,12,128,64]{3,2,1,0:T(8,128)} %get-tuple-element.546, f32[6,256,12]{1,2,0:T(8,128)S(1)} %copy-done.30, f32[6,256,12,64]{1,0,3,2:T(8,128)} %reshape.302), kind=kOutput, calls=%fused_computation.129 | convolution fusion | flops 1813118976 | bytes 7938048 | tf_op jit(solution)/shard_map/transpose(jvp(cin,chnp->cihp))/dot_general | solution.py:60
  262.4 5.1 multiply_reduce_fusion.8
  267.5 4.9 fusion.70
  275.7 45.6 %while.35 = (s32[]{:T(128)}, f32[12,128,64]{2,1,0:T(8,128)}, f32[6,12,128,64]{3,2,1,0:T(8,128)}, f32[6,12]{1,0:T(8,128)}, f32[6,12,128,64]{2,3,1,0:T(8,128)}, /*...) while((s32[]{:T(128)}, f32[12,128,64]{2,1,0:T(8,128)}, ...), condition=%wide.region_12.13_spmd.clone, body=%wide.region_10.12_spmd.clone.sunk | while | flops 589816 | bytes 4719024 | solution.py:58
  321.3 18.7 %fusion.80 = f32[6,256,128]{2,1,0:T(8,128)S(1)} fusion(f32[6,12,128,64]{3,2,1,0:T(8,128)} %get-tuple-element.193, f32[6,256,12,64]{1,3,2,0:T(8,128)} %copy.178, f32[6,256,12]{1,2,0:T(8,128)} %copy-done.28), kind=kOutput, calls=%fused_computation.130 | convolution fusion | flops 1813118976 | bytes 7938048 | tf_op jit(solution)/shard_map/transpose(jvp(cjn,cjhp->chnp))/dot_general | solution.py:49
  340.1 8.7 multiply_reduce_fusion.9
  348.9 24.1 %fusion.11 = (f32[6,12,256]{2,1,0:T(8,128)}, f32[6,12,256]{2,1,0:T(8,128)}, f32[6,12,256]{2,1,0:T(8,128)}, f32[6,256,256]{2,1,0:T(8,128)S(1)}) fusion(f32[6,12,256]{2,1,0:T(8,128)S(1)} %bitcast.261, f32[6,256,256]{2,1,0:T(8,128)S(1)} %copy-done.26, f32[6,12,256]{2,1,0:T(8,128)S(1)} %copy-done.25, pred[6,256,256]{2,1,0:T(8,128)(4,1)S(1)} %copy-done.35, ...), kind=kOutput, calls=%fused_computation.31 | convolution fusion | flops 3694209024 | bytes 10985472 | tf_op jit(solution)/shard_map/transpose(jvp(chij,cjhp->cihp))/dot_general | solution.py:45
  379.6 14.9 %reduce-window.16 = f32[6,12,2,128]{3,1,2,0:T(8,128)S(1)} reduce-window(f32[6,12,2,128]{3,1,2,0:T(8,128)S(1)} %copy.201, f32[]{:T(128)} %constant.111.clone.1), window={size=1x1x1x128 pad=0_0x0_0x0_0x0_127}, to_apply=%region_19.20 | reduce-window | flops 2340864 | bytes 147460 | tf_op jit(solution)/shard_map/reduce-window.2
  395.1 24.2 %bitcast_add_fusion.2 = f32[6,256,12,64]{1,3,2,0:T(8,128)} fusion(f32[6,256,12,64]{1,3,2,0:T(8,128)} %get-tuple-element.427, f32[12]{0:T(128)} %param.34, f32[6,256,12]{1,2,0:T(8,128)S(1)} %copy-done.29, f32[6,12,256]{2,1,0:T(8,128)} %bitcast.259, f32[6,256,256]{2,1,0:T(8,128)} %fusion.119, f32[6,12,256]{2,1,0:T(8,128)S(1)} %copy-done.25, ...), kind=kOutput, calls=%fused_computation.62 | convolution fusion | flops 3652190208 | bytes 21061680 | tf_op jit(solution)/shard_map/transpose(jvp(chij,cjhp->cihp))/dot_general | solution.py:45
  419.3 10.7 copy.221
  430.1 10.0 reshape.330
  440.1 9.9 multiply_reduce_fusion.7
  458.4 6.5 fusion.122
  465.0 4.0 fusion.121
  470.5 5.2 convolution_add_fusion.1
  475.8 10.5 fusion.106
  486.6 3.9 fusion.97
  490.5 8.6 fusion.124
  499.1 5.6 fusion.123
  504.8 6.5 fusion.63
  511.2 160.3 %all-reduce.34.cloned.1.call-done = (f32[1536,1536]{1,0:T(8,128)}, f32[1536,256]{1,0:T(8,128)}) async-done(((f32[1536,1536]{1,0:T(8,128)}, f32[1536,256]{1,0:T(8,128)}), (f32[1536,1536]{1,0:T(8,128)}, f32[1536,256]{1,0:T(8,128)})) %all-reduce.34.cloned.1.call-update) | async-done | bytes 11010064 | tf_op jit(solution)/shard_map/psum | solution.py:149
  682.1 15.2 %fusion.21 = (f32[1536]{0:T(1024)S(1)}, f32[1536]{0:T(1024)S(1)}, f32[1536,1536]{1,0:T(8,128)}) fusion(bf16[1536,1536]{1,0:T(8,128)(2,1)} %param.21, f32[1536]{0:T(1024)S(1)} %copy-done.48, f32[1536]{0:T(1024)S(1)} %copy-done.55, f32[1536,1536]{1,0:T(8,128)} %get-tuple-element.361, bf16[1536,256]{1,0:T(8,128)(2,1)S(1)} %get-tuple-element.395, ...), kind=kOutput, calls=%fused_computation.43 | convolution fusion | flops 1226830848 | bytes 25190400 | tf_op jit(solution)/shard_map/dot_general | solution.py:72
  697.4 38.7 %all-reduce.26 = (f32[1536]{0:T(1024)}, f32[4,768]{1,0:T(4,128)}, f32[4,256]{1,0:T(4,128)}, f32[768]{0:T(1024)}, f32[256]{0:T(256)}, /*index=5*/f32[12]{0:T(128)}, f32[12]{0:T(128)}, f32[12]{0:T(128)}, f32[768]{0:T(1024)}) all-reduce(f32[1536]{0:T(1024)S(1)} %get-tuple-element.309, ...), channel_id=1, replica_groups=mesh['dp'=8,'tensor'=4] {'dp'}, use_global_device_ids=true, to_apply=%region_26.27 | all-reduce | flops 7460 | bytes 59680 | tf_op jit(solution)/shard_map/psum | solution.py:164
  736.1 164.4 %all-gather.3.cloned.1.call-done = f32[6144,1536]{1,0:T(8,128)} async-done(((f32[1536,1536]{1,0:T(8,128)}), f32[6144,1536]{1,0:T(8,128)}) %all-gather.3.cloned.1.call-update) | async-done | bytes 37748752 | tf_op jit(solution)/shard_map/all_gather | solution.py:127
  900.5 19.6 %reduce_sum.274 = f32[1536,1536]{1,0:T(8,128)} reduce(f32[4,1536,1536]{2,1,0:T(8,128)} %bitcast.226, f32[]{:T(128)} %constant.111.clone.1), dimensions={0}, to_apply=%region_7.8 | reduce | flops 7077888 | bytes 47185924 | tf_op jit(solution)/shard_map/reduce_sum | solution.py:127
  920.1 16.3 %fusion.13 = (f32[1536,1536]{1,0:T(8,128)}, bf16[1536,1536]{1,0:T(8,128)(2,1)}) fusion(bf16[1536,1536]{1,0:T(8,128)(2,1)} %param.37, bf16[1536,1536]{1,0:T(8,128)(2,1)} %param.21, f32[1536,1536]{1,0:T(8,128)} %get-tuple-element.428, f32[1536]{0:T(1024)S(1)} %broadcast_multiply_fusion.8, f32[1536]{0:T(1024)S(1)} %copy-done.68, f32[1536]{0:T(1024)S(1)} %copy-done.55, ...), kind=kLoop, calls=%fused_computation.35 | loop fusion | flops 25952256 | bytes 42498048 | tf_op jit(solution)/shard_map/sub | solution.py:156
  936.4 455.0 %all-reduce.32.cloned.1.call-done = (f32[1536,768]{1,0:T(8,128)}, f32[1536,768]{1,0:T(8,128)}, f32[1536,12]{0,1:T(8,128)}, f32[1536,256]{1,0:T(8,128)}, f32[768,1536]{1,0:T(8,128)}) async-done(((f32[1536,768]{1,0:T(8,128)}, f32[1536,768]{1,0:T(8,128)}, f32[1536,12]{0,1:T(8,128)}, f32[1536,256]{1,0:T(8,128)}, f32[768,1536]{1,0:T(8,128)}), (f32[1536,768]{1,0:T(8,128)}, f32[1536,768]{1,0:T(8,128)}, ...) | async-done | bytes 15802384 | tf_op jit(solution)/shard_map/psum | solution.py:164
  1391.4 5.2 copy.308
  (402 shorter events, 157.7 us)
Async XLA Ops:
  7.2 173.8 %copy-start = (bf16[1536,768]{1,0:T(8,128)(2,1)S(1)}, bf16[1536,768]{1,0:T(8,128)(2,1)}, u32[]{:S(2)}) copy-start(bf16[1536,768]{1,0:T(8,128)(2,1)} %param.24) | copy-start | bytes 7077892
  7.2 664.3 %all-reduce.34.cloned.1.call-start = ((), (), s32[]{:S(2)}) async-start(), calls=%async_computation.2 | async-start | bytes 22020096 | tf_op jit(solution)/shard_map/psum | solution.py:149
  19.0 46.1 %copy-start.37 = (f32[1536]{0:T(1024)}, f32[1536]{0:T(1024)S(1)}, u32[]{:S(2)}) copy-start(f32[1536]{0:T(1024)S(1)} %get-tuple-element.414) | copy-start | bytes 18436
  19.0 46.1 %copy-start.39 = (f32[1536]{0:T(1024)}, f32[1536]{0:T(1024)S(1)}, u32[]{:S(2)}) copy-start(f32[1536]{0:T(1024)S(1)} %get-tuple-element.412) | copy-start | bytes 18436
  19.0 46.2 %copy-start.41 = (f32[1536]{0:T(1024)}, f32[1536]{0:T(1024)S(1)}, u32[]{:S(2)}) copy-start(f32[1536]{0:T(1024)S(1)} %get-tuple-element.413) | copy-start | bytes 18436
  34.0 8.8 copy-start.91
  34.0 8.8 copy-start.45
  34.0 8.8 copy-start.87
  51.2 19.3 %copy-start.23 = (f32[6,12,256]{2,1,0:T(8,128)}, f32[6,12,256]{2,1,0:T(8,128)S(1)}, u32[]{:S(2)}) copy-start(f32[6,12,256]{2,1,0:T(8,128)S(1)} %reduce_window_sum.39) | copy-start | bytes 221188
  51.4 19.1 %copy-start.17 = (f32[6,256,12]{1,0,2:T(8,128)}, f32[6,256,12]{1,0,2:T(8,128)S(1)}, u32[]{:S(2)}) copy-start(f32[6,256,12]{1,0,2:T(8,128)S(1)} %reshape.299) | copy-start | bytes 221188
  51.4 9.9 copy-start.31
  68.8 9.0 copy-start.10
  69.7 8.1 copy-start.49
  69.7 8.1 copy-start.58
  133.3 8.5 copy-start.24
  133.3 8.5 copy-start.30
  133.3 8.5 copy-start.51
  133.3 8.5 copy-start.90
  181.0 18.8 %copy-start.44 = (f32[768]{0:T(1024)S(1)}, f32[768]{0:T(1024)}, u32[]{:S(2)}) copy-start(f32[768]{0:T(1024)} %param.35) | copy-start | bytes 9220
  181.0 18.8 %copy-start.56 = (f32[1536]{0:T(1024)S(1)}, f32[1536]{0:T(1024)}, u32[]{:S(2)}) copy-start(f32[1536]{0:T(1024)} %get-tuple-element.411) | copy-start | bytes 18436
  242.8 19.6 %copy-start.4 = (f32[6,256,12,64]{1,0,3,2:T(8,128)S(1)}, f32[6,256,12,64]{1,0,3,2:T(8,128)}, u32[]{:S(2)}) copy-start(f32[6,256,12,64]{1,0,3,2:T(8,128)} %reshape.302) | copy-start | bytes 14155780
  321.3 18.7 %copy-start.7 = (f32[6,12,128,64]{3,2,1,0:T(8,128)S(1)}, f32[6,12,128,64]{3,2,1,0:T(8,128)}, u32[]{:S(2)}) copy-start(f32[6,12,128,64]{3,2,1,0:T(8,128)} %get-tuple-element.193) | copy-start | bytes 7077892
  321.3 18.7 %copy-start.12 = (bf16[1536,128]{1,0:T(8,128)(2,1)S(1)}, bf16[1536,128]{1,0:T(8,128)(2,1)}, u32[]{:S(2)}) copy-start(bf16[1536,128]{1,0:T(8,128)(2,1)} %copy-done.10) | copy-start | bytes 1179652
  321.3 27.5 %slice-start.2 = ((s8[6291456]{0:T(1024)(128)(4,1)}), s8[4194304]{0:T(1024)(128)(4,1)S(1)}, s32[]{:S(2)}) async-start(s8[6291456]{0:T(1024)(128)(4,1)} %bitcast.217), calls=%async_computation.5 | async-start | bytes 8388608
  340.0 8.8 slice-start.3
  340.0 8.8 copy-start.22
  340.0 8.8 copy-start.25
  340.0 8.8 copy-start.26
  340.0 8.8 copy-start.35
  340.1 8.8 copy-start.52
  348.9 24.2 %copy-start.14 = (f32[6,256,128]{2,1,0:T(8,128)S(1)}, f32[6,256,128]{2,1,0:T(8,128)}, u32[]{:S(2)}) copy-start(f32[6,256,128]{2,1,0:T(8,128)} %fusion.77) | copy-start | bytes 2359300
  348.9 26.0 %copy-start.9 = (bf16[1536,128]{1,0:T(8,128)(2,1)S(1)}, bf16[1536,128]{1,0:T(8,128)(2,1)}, u32[]{:S(2)}) copy-start(bf16[1536,128]{1,0:T(8,128)(2,1)} %get-tuple-element.399) | copy-start | bytes 1179652
  373.1 22.0 %copy-start.29 = (f32[6,256,12]{1,2,0:T(8,128)S(1)}, f32[6,256,12]{1,2,0:T(8,128)}, u32[]{:S(2)}) copy-start(f32[6,256,12]{1,2,0:T(8,128)} %copy-done.28) | copy-start | bytes 221188
  430.1 10.0 copy-start.38
  430.1 19.9 %slice-start = ((s8[4718592]{0:T(1024)(128)(4,1)}), s8[524288]{0:T(1024)(128)(4,1)S(1)}, s32[]{:S(2)}) async-start(s8[4718592]{0:T(1024)(128)(4,1)} %bitcast.206), calls=%async_computation.3 | async-start | bytes 1048576
  440.1 9.9 slice-start.1
  440.1 9.9 copy-start.40
  440.1 9.9 copy-start.42
  475.7 424.8 %all-gather.3.cloned.1.call-start = ((), (), s32[]{:S(2)}) async-start(), calls=%async_computation | async-start | bytes 47185920 | tf_op jit(solution)/shard_map/all_gather | solution.py:127
  486.3 12.8 slice-start.6
  486.3 905.0 %all-reduce.32.cloned.1.call-start = ((), (), s32[]{:S(2)}) async-start(), calls=%async_computation.1 | async-start | bytes 31653888 | tf_op jit(solution)/shard_map/psum | solution.py:164
  490.5 8.6 slice-start.7
  490.5 8.6 copy-start.21
  490.5 14.3 %slice-start.10 = ((s8[4718592]{0:T(1024)(128)(4,1)}), s8[4194304]{0:T(1024)(128)(4,1)S(1)}, s32[]{:S(2)}) async-start(s8[4718592]{0:T(1024)(128)(4,1)} %bitcast.227), calls=%async_computation.13 | async-start | bytes 8388608
  490.5 14.3 %slice-start.14 = ((s8[4718592]{0:T(1024)(128)(4,1)}), s8[4194304]{0:T(1024)(128)(4,1)S(1)}, s32[]{:S(2)}) async-start(s8[4718592]{0:T(1024)(128)(4,1)} %bitcast.233), calls=%async_computation.17 | async-start | bytes 8388608
  682.1 15.3 %copy-start.85 = (f32[768]{0:T(1024)S(1)}, f32[768]{0:T(1024)}, u32[]{:S(2)}) copy-start(f32[768]{0:T(1024)} %get-tuple-element.311) | copy-start | bytes 9220
  900.5 19.6 %copy-start.68 = (f32[1536]{0:T(1024)S(1)}, f32[1536]{0:T(1024)}, u32[]{:S(2)}) copy-start(f32[1536]{0:T(1024)} %get-tuple-element.407) | copy-start | bytes 18436
  1391.4 10.0 slice-start.16
  (66 other events, 260.5 us)
Sparse Core Ops, SparseCore 0:
  475.8 195.6 all-reduce.33
  673.1 227.3 all-gather.2
  906.8 484.5 all-reduce.31
